TPU v7x, 256 devices: a whole 4x4x8 slice. The times are simulated.
256 devices in a mesh: dir: 8 (over x_hi, y), space: 32 (over z, x_lo, core).
Axes of the slice: x: 4 (x_hi: 2, x_lo: 2; x = x_hi * 2 + x_lo), y: 4, z: 8, core: 2. Of those that a mesh axis runs over, the one named last changes fastest.
Arguments:
- directions: float32 [16, 2048, 4096], P('dir', 'space'), may hold values from -6.3 to 6.3
- pool: float32 [16, 2048, 4096], P('dir', 'space'), may hold values from -6 to 6
- owners: int32 [2, 2], replicated, may hold values from 0 to 15, as said below
- window_steps: int32 [2], replicated, may hold values from 0 to 511
- diffusion: float32 [512], replicated, may hold values from 0.02 to 0.2
- obs_weight: float32 [2048, 4096], P('space'), may hold values from 0.5 to 2
- prior_diag: float32 [2048, 4096], P('space'), may hold values from 0.1 to 1
Outputs:
- product: float32 [16, 2048, 4096], P('dir', 'space')
- curvature: float32 [16], P('dir')
Inputs may be any that keep to these rules, and one draw needn't show every extreme that they name: `owners`: the 4 entries are distinct; 0 and 15 are always among them.
All inputs are finite; a program needn't handle non-finite values.
Results may differ from a plain program's by a relative error of at most 0.00002.
Values sent between devices are 32-bit elements; how exact they have to be, the bound alone decides.
No kernel may reach another device: no remote copies, remote signals or barrier semaphores. Data moves between devices by JAX's collectives and lax.ppermute only.
A program may use at most 64 MiB of HBM per device.

v0:
```python
import jax
import jax.numpy as jnp
from jax import lax
from jax.sharding import PartitionSpec as P

STEPS = 2


advection_rate = 0.25


def broadcast(block, axis, source):
    block = jnp.where(lax.axis_index(axis) == source, block, jnp.zeros_like(block))
    return lax.psum(block, axis)


def padded_2(array, sides, width):
    for axis, dim in sides:
        peers, length = (lax.axis_size(axis), array.shape[dim])
        up = [(i, (i + 1) % peers) for i in range(peers - 1)]
        down = [(j, i) for i, j in up]
        last = lax.slice_in_dim(array, length - width, length, axis=dim)
        leading = lax.slice_in_dim(array, 0, width, axis=dim)
        before = lax.ppermute(last, axis, up)
        after = lax.ppermute(leading, axis, down)
        array = jnp.concatenate([before, array, after], axis=dim)
    return array


def stencil_parts(padded):
    widened = jnp.pad(padded, [(0, 0)] * (padded.ndim - 1) + [(1, 1)])
    centre = widened[..., 1:-1, 1:-1]
    row_above = widened[..., 2:, 1:-1]
    row_below = widened[..., :-2, 1:-1]
    col_right = widened[..., 1:-1, 2:]
    col_left = widened[..., 1:-1, :-2]
    laplace = row_above + row_below + col_right + col_left - 4.0 * centre
    central = 0.5 * (row_above - row_below + col_right - col_left)
    return (laplace, central)


def per_device(directions, pool, owners, window_steps, diffusion, obs_weight, prior_diag):
    table_index = jnp.arange(diffusion.shape[0], dtype=jnp.int32)
    rate_list = jnp.sum(
        jnp.where(table_index[None, :] == window_steps[:, None], diffusion[None, :], 0.0), axis=1
    )
    local_slots = pool.shape[0]

    def checkpoint(owner_index):
        held = lax.dynamic_index_in_dim(pool, owner_index % local_slots, 0, keepdims=False)
        return broadcast(held, "dir", owner_index // local_slots)

    current = directions
    history = []
    velocity = []
    for moment in range(STEPS):
        history.append(current)
        velocity_now = checkpoint(owners[0, moment])
        velocity.append(velocity_now)
        padded_state, padded_moved = (
            padded_2(current, (("space", 1),), 1),
            padded_2(velocity_now[None] * current, (("space", 1),), 1),
        )
        diffused = stencil_parts(padded_state)[0]
        advected = stencil_parts(padded_moved)[1]
        current = current + rate_list[moment] * diffused - advection_rate * advected
    adjoint = obs_weight[None] * current
    for moment in reversed(range(STEPS)):
        stored_adjoint = checkpoint(owners[1, moment])
        padded_adjoint, padded_stored = (
            padded_2(adjoint, (("space", 1),), 1),
            padded_2(stored_adjoint[None], (("space", 1),), 1),
        )
        adjoint_diffused, adjoint_slope = stencil_parts(padded_adjoint)
        state_slope = stencil_parts(padded_stored)[1]
        adjoint = (
            adjoint
            + rate_list[moment] * adjoint_diffused
            + advection_rate * velocity[moment][None] * adjoint_slope
            + advection_rate * history[moment] * state_slope
        )
    product = adjoint + prior_diag[None] * directions
    partial_sums = jnp.sum(directions * product, axis=(1, 2))
    summed = lax.psum(partial_sums, "space")
    cells = directions.shape[1] * lax.axis_size("space") * directions.shape[2]
    return (product, summed / cells)


def solution(mesh):
    return jax.shard_map(
        per_device,
        mesh=mesh,
        in_specs=(
            P("dir", "space", None),
            P("dir", "space", None),
            P(),
            P(),
            P(),
            P("space", None),
            P("space", None),
        ),
        out_specs=(P("dir", "space", None), P("dir")),
        check_vma=False,
    )
```

profile of v0, /device:TPU:129, one launch (start us, length us, event | category | flops | bytes accessed | tf_op | source)
XLA Modules:
  0.0 280.1 jit_solution(9238986769812587617)
XLA Ops:
  7.2 1.5 fusion.33
  18.8 4.3 %dynamic-slice_select_fusion = (f32[1,64,4096]{2,1,0:T(8,128)}, f32[64,4096]{1,0:T(8,128)}, f32[64,4096]{1,0:T(8,128)}, f32[1,64,4096]{2,1,0:T(8,128)}) fusion(f32[2,64,4096]{2,1,0:T(8,128)} %param.8, s32[]{:T(128)S(6)} %select_n.109, pred[]{:T(512)S(6)} %eq.36, s32[]{:T(128)S(6)} %select_n.97, pred[]{:T(512)S(6)} %eq.34, s32[]{:T(128)S(6)} %select_n.91, ...), kind=kLoop, calls=%fused_computation.74 | loop fusion | flops 1048576 | bytes 8388628 | tf_op jit(solution)/shard_map/jit(_where)/select_n | solution.py:13
  23.1 1.6 copy-done
  24.7 2.6 collective-permute-start
  27.3 3.0 %collective-permute-start.1 = (f32[2,1,4096]{2,1,0:T(1,128)S(1)}, f32[2,1,4096]{2,1,0:T(1,128)S(1)}, u32[]{:S(2)}, u32[]{:S(2)}) collective-permute-start(f32[2,1,4096]{2,1,0:T(1,128)S(1)} %get-tuple-element.18), channel_id=1, source_target_pairs={{0,1},{1,2},{2,3},{3,4},{4,5},{5,6},{6,7},{7,8},{8,9},{9,10},{10,1... | collective-permute-start | bytes 98312 | tf_op jit(solution)/shard_map/ppermute | solution.py:24
  31.3 2.3 select_maximum_fusion.10
  33.6 106.2 %all-reduce.11.cloned.1.call-done = (f32[64,4096]{1,0:T(8,128)}, f32[64,4096]{1,0:T(8,128)}, f32[1,64,4096]{2,1,0:T(8,128)}, f32[1,64,4096]{2,1,0:T(8,128)}) async-done(((f32[64,4096]{1,0:T(8,128)}, f32[64,4096]{1,0:T(8,128)}, f32[1,64,4096]{2,1,0:T(8,128)}, f32[1,64,4096]{2,1,0:T(8,128)}), (f32[64,4096]{1,0:T(8,128)}, f32[64,4096]{1,0:T(8,128)}, f32[1,64,4096]{2,1,0:T(8,128)}, ...) | async-done | bytes 4194320 | tf_op jit(solution)/shard_map/psum | solution.py:14
  139.8 1.5 broadcast_multiply_fusion.1
  141.5 2.9 %collective-permute-start.2 = (f32[2,1,4096]{2,1,0:T(1,128)S(1)}, f32[2,1,4096]{2,1,0:T(1,128)S(1)}, u32[]{:S(2)}, u32[]{:S(2)}) collective-permute-start(f32[2,1,4096]{2,1,0:T(1,128)S(1)} %get-tuple-element.21), channel_id=1, source_target_pairs={{1,0},{2,1},{3,2},{4,3},{5,4},{6,5},{7,6},{8,7},{9,8},{10,9},{11,1... | collective-permute-start | bytes 98312 | tf_op jit(solution)/shard_map/ppermute | solution.py:25
  144.4 2.8 %collective-permute-start.3 = (f32[2,1,4096]{2,1,0:T(1,128)S(1)}, f32[2,1,4096]{2,1,0:T(1,128)S(1)}, u32[]{:S(2)}, u32[]{:S(2)}) collective-permute-start(f32[2,1,4096]{2,1,0:T(1,128)S(1)} %get-tuple-element.20), channel_id=1, source_target_pairs={{0,1},{1,2},{2,3},{3,4},{4,5},{5,6},{6,7},{7,8},{8,9},{9,10},{10,1... | collective-permute-start | bytes 98312 | tf_op jit(solution)/shard_map/ppermute | solution.py:24
  147.3 1.9 collective-permute-start.10
  149.2 3.6 %collective-permute-start.11 = (f32[1,1,4096]{2,1,0:T(1,128)S(1)}, f32[1,1,4096]{2,1,0:T(1,128)S(1)}, u32[]{:S(2)}, u32[]{:S(2)}) collective-permute-start(f32[1,1,4096]{2,1,0:T(1,128)S(1)} %get-tuple-element.26), channel_id=1, source_target_pairs={{0,1},{1,2},{2,3},{3,4},{4,5},{5,6},{6,7},{7,8},{8,9},{9,10},{10,1... | collective-permute-start | bytes 49160 | tf_op jit(solution)/shard_map/ppermute | solution.py:24
  153.0 3.1 %collective-permute-start.14 = (f32[1,1,4096]{2,1,0:T(1,128)S(1)}, f32[1,1,4096]{2,1,0:T(1,128)S(1)}, u32[]{:S(2)}, u32[]{:S(2)}) collective-permute-start(f32[1,1,4096]{2,1,0:T(1,128)S(1)} %get-tuple-element.29), channel_id=1, source_target_pairs={{1,0},{2,1},{3,2},{4,3},{5,4},{6,5},{7,6},{8,7},{9,8},{10,9},{11,1... | collective-permute-start | bytes 49160 | tf_op jit(solution)/shard_map/ppermute | solution.py:25
  156.1 2.4 collective-permute-start.15
  159.6 0.8 select_maximum_fusion.8
  161.3 3.6 %broadcast_multiply_fusion = (f32[2,64,4096]{2,1,0:T(8,128)S(1)}, f32[2,64,4096]{2,1,0:T(8,128)S(1)}) fusion(f32[64,4096]{1,0:T(8,128)S(1)} %copy-done.5, f32[2,66,4098]{2,1,0:T(8,128)S(1)} %select_maximum_fusion.8, f32[2,64,4096]{2,1,0:T(8,128)S(1)} %broadcast_multiply_fusion.1, f32[2,1,4096]{2,1,0:T(1,128)S(1)} %collective-permute-done.3, ...), kind=kLoop, calls=%fused_computation.76 | loop fusion | flops 8912896 | bytes 17956868 | tf_op jit(solution)/shard_map/mul | solution.py:62
  164.9 5.2 %collective-permute-start.4 = (f32[2,1,4096]{2,1,0:T(1,128)S(1)}, f32[2,1,4096]{2,1,0:T(1,128)S(1)}, u32[]{:S(2)}, u32[]{:S(2)}) collective-permute-start(f32[2,1,4096]{2,1,0:T(1,128)S(1)} %get-tuple-element.15), channel_id=1, source_target_pairs={{1,0},{2,1},{3,2},{4,3},{5,4},{6,5},{7,6},{8,7},{9,8},{10,9},{11,1... | collective-permute-start | bytes 98312 | tf_op jit(solution)/shard_map/ppermute | solution.py:25
  170.2 1.9 collective-permute-start.5
  172.2 5.8 %collective-permute-start.6 = (f32[2,1,4096]{2,1,0:T(1,128)S(1)}, f32[2,1,4096]{2,1,0:T(1,128)S(1)}, u32[]{:S(2)}, u32[]{:S(2)}) collective-permute-start(f32[2,1,4096]{2,1,0:T(1,128)S(1)} %get-tuple-element.17), channel_id=1, source_target_pairs={{1,0},{2,1},{3,2},{4,3},{5,4},{6,5},{7,6},{8,7},{9,8},{10,9},{11,1... | collective-permute-start | bytes 98312 | tf_op jit(solution)/shard_map/ppermute | solution.py:25
  177.9 1.9 collective-permute-start.7
  179.9 0.8 select_maximum_fusion.6
  180.7 3.6 %collective-permute-done.7 = f32[2,1,4096]{2,1,0:T(1,128)S(1)} collective-permute-done((f32[2,1,4096]{2,1,0:T(1,128)S(1)}, f32[2,1,4096]{2,1,0:T(1,128)S(1)}, u32[]{:S(2)}, u32[]{:S(2)}) %collective-permute-start.7) | collective-permute-done | bytes 32800 | tf_op jit(solution)/shard_map/ppermute | solution.py:24
  184.4 0.8 select_maximum_fusion.4
  185.2 3.7 %fusion.3 = f32[2,64,4096]{2,1,0:T(8,128)S(1)} fusion(f32[2,66,4098]{2,1,0:T(8,128)S(1)} %select_maximum_fusion.4, f32[2,64,4096]{2,1,0:T(8,128)S(1)} %get-tuple-element.8, f32[2,1,4096]{2,1,0:T(1,128)S(1)} %collective-permute-done.7, f32[2,1,4096]{2,1,0:T(1,128)S(1)} %collective-permute-done.6, f32[2,64,4096]{2,1,0:T(8,128)S(1)} %get-tuple-element.9, ...), kind=kLoop, calls=%fused_computation.22 | loop fusion | flops 8912896 | bytes 15859716 | tf_op jit(solution)/shard_map/mul | solution.py:67
  189.0 6.6 %collective-permute-start.8 = (f32[2,1,4096]{2,1,0:T(1,128)S(1)}, f32[2,1,4096]{2,1,0:T(1,128)S(1)}, u32[]{:S(2)}, u32[]{:S(2)}) collective-permute-start(f32[2,1,4096]{2,1,0:T(1,128)S(1)} %get-tuple-element.13), channel_id=1, source_target_pairs={{1,0},{2,1},{3,2},{4,3},{5,4},{6,5},{7,6},{8,7},{9,8},{10,9},{11,1... | collective-permute-start | bytes 98312 | tf_op jit(solution)/shard_map/ppermute | solution.py:25
  195.7 2.1 collective-permute-start.9
  199.6 2.5 multiply_add_fusion.1
  202.2 6.2 %collective-permute-start.12 = (f32[2,1,4096]{2,1,0:T(1,128)S(1)}, f32[2,1,4096]{2,1,0:T(1,128)S(1)}, u32[]{:S(2)}, u32[]{:S(2)}) collective-permute-start(f32[2,1,4096]{2,1,0:T(1,128)S(1)} %get-tuple-element.11), channel_id=1, source_target_pairs={{1,0},{2,1},{3,2},{4,3},{5,4},{6,5},{7,6},{8,7},{9,8},{10,9},{11,1... | collective-permute-start | bytes 98312 | tf_op jit(solution)/shard_map/ppermute | solution.py:25
  208.4 1.9 collective-permute-start.13
  211.5 0.8 select_maximum_fusion
  212.4 3.8 %multiply_reduce_fusion = (f32[2]{0:T(128)S(1)}, f32[2,64,4096]{2,1,0:T(8,128)}) fusion(f32[2,64,4096]{2,1,0:T(8,128)S(1)} %copy-done, f32[64,4096]{1,0:T(8,128)S(1)} %copy-done.7, f32[64,4096]{1,0:T(8,128)S(1)} %fusion.18, f32[64,4096]{1,0:T(8,128)S(1)} %broadcast_multiply_fusion.2, f32[2,64,4096]{2,1,0:T(8,128)S(1)} %multiply_add_fusion.1, ...), kind=kLoop, calls=%fused_computation.50 | loop fusion | flops 10485758 | bytes 13697036 | tf_op jit(solution)/shard_map/reduce_sum | solution.py:83
  216.2 56.6 %psum.39 = f32[2]{0:T(128)S(1)} all-reduce(f32[2]{0:T(128)S(1)} %get-tuple-element.6), channel_id=1, replica_groups=mesh['dir'=8,'space'=32] {'space'}, use_global_device_ids=true, to_apply=%region_6.7 | all-reduce | flops 2 | bytes 16 | tf_op jit(solution)/shard_map/psum | solution.py:84
  (54 shorter events, 6.8 us)
Async XLA Ops:
  7.2 132.6 %all-reduce.11.cloned.1.call-start = ((), (), s32[]{:S(2)}) async-start(), calls=%async_computation | async-start | bytes 8388608 | tf_op jit(solution)/shard_map/psum | solution.py:14
  23.1 1.6 copy-start
  23.1 7.3 %copy-start.8 = (f32[512]{0:T(512)S(1)}, f32[512]{0:T(512)}, u32[]{:S(2)}) copy-start(f32[512]{0:T(512)} %param.11) | copy-start | bytes 6148
  23.1 7.3 %copy-start.9 = (s32[2]{0:T(128)S(1)}, s32[2]{0:T(128)}, u32[]{:S(2)}) copy-start(s32[2]{0:T(128)} %param.10) | copy-start | bytes 28
  24.7 6.4 %collective-permute-start = (f32[2,1,4096]{2,1,0:T(1,128)S(1)}, f32[2,1,4096]{2,1,0:T(1,128)S(1)}, u32[]{:S(2)}, u32[]{:S(2)}) collective-permute-start(f32[2,1,4096]{2,1,0:T(1,128)S(1)} %get-tuple-element.19), channel_id=1, source_target_pairs={{1,0},{2,1},{3,2},{4,3},{5,4},{6,5},{7,6},{8,7},{9,8},{10,9},{11,1... | collective-permute-start | bytes 98312 | tf_op jit(solution)/shard_map/ppermute | solution.py:25
  27.3 4.0 %collective-permute-start.1 = (f32[2,1,4096]{2,1,0:T(1,128)S(1)}, f32[2,1,4096]{2,1,0:T(1,128)S(1)}, u32[]{:S(2)}, u32[]{:S(2)}) collective-permute-start(f32[2,1,4096]{2,1,0:T(1,128)S(1)} %get-tuple-element.18), channel_id=1, source_target_pairs={{0,1},{1,2},{2,3},{3,4},{4,5},{5,6},{6,7},{7,8},{8,9},{9,10},{10,1... | collective-permute-start | bytes 98312 | tf_op jit(solution)/shard_map/ppermute | solution.py:24
  139.8 1.6 copy-start.4
  139.8 13.1 %copy-start.5 = (f32[64,4096]{1,0:T(8,128)S(1)}, f32[64,4096]{1,0:T(8,128)}, u32[]{:S(2)}) copy-start(f32[64,4096]{1,0:T(8,128)} %get-tuple-element.3) | copy-start | bytes 3145732
  141.4 5.9 %copy-start.3 = (f32[1,64,4096]{2,1,0:T(8,128)S(1)}, f32[1,64,4096]{2,1,0:T(8,128)}, u32[]{:S(2)}) copy-start(f32[1,64,4096]{2,1,0:T(8,128)} %get-tuple-element.4) | copy-start | bytes 3145732
  141.4 11.6 %copy-start.2 = (f32[1,64,4096]{2,1,0:T(8,128)S(1)}, f32[1,64,4096]{2,1,0:T(8,128)}, u32[]{:S(2)}) copy-start(f32[1,64,4096]{2,1,0:T(8,128)} %get-tuple-element.5) | copy-start | bytes 3145732
  141.5 18.1 %collective-permute-start.2 = (f32[2,1,4096]{2,1,0:T(1,128)S(1)}, f32[2,1,4096]{2,1,0:T(1,128)S(1)}, u32[]{:S(2)}, u32[]{:S(2)}) collective-permute-start(f32[2,1,4096]{2,1,0:T(1,128)S(1)} %get-tuple-element.21), channel_id=1, source_target_pairs={{1,0},{2,1},{3,2},{4,3},{5,4},{6,5},{7,6},{8,7},{9,8},{10,9},{11,1... | collective-permute-start | bytes 98312 | tf_op jit(solution)/shard_map/ppermute | solution.py:25
  144.4 15.2 %collective-permute-start.3 = (f32[2,1,4096]{2,1,0:T(1,128)S(1)}, f32[2,1,4096]{2,1,0:T(1,128)S(1)}, u32[]{:S(2)}, u32[]{:S(2)}) collective-permute-start(f32[2,1,4096]{2,1,0:T(1,128)S(1)} %get-tuple-element.20), channel_id=1, source_target_pairs={{0,1},{1,2},{2,3},{3,4},{4,5},{5,6},{6,7},{7,8},{8,9},{9,10},{10,1... | collective-permute-start | bytes 98312 | tf_op jit(solution)/shard_map/ppermute | solution.py:24
  147.3 8.9 %collective-permute-start.10 = (f32[1,1,4096]{2,1,0:T(1,128)S(1)}, f32[1,1,4096]{2,1,0:T(1,128)S(1)}, u32[]{:S(2)}, u32[]{:S(2)}) collective-permute-start(f32[1,1,4096]{2,1,0:T(1,128)S(1)} %get-tuple-element.27), channel_id=1, source_target_pairs={{1,0},{2,1},{3,2},{4,3},{5,4},{6,5},{7,6},{8,7},{9,8},{10,9},{11,1... | collective-permute-start | bytes 49160 | tf_op jit(solution)/shard_map/ppermute | solution.py:25
  149.2 9.4 %collective-permute-start.11 = (f32[1,1,4096]{2,1,0:T(1,128)S(1)}, f32[1,1,4096]{2,1,0:T(1,128)S(1)}, u32[]{:S(2)}, u32[]{:S(2)}) collective-permute-start(f32[1,1,4096]{2,1,0:T(1,128)S(1)} %get-tuple-element.26), channel_id=1, source_target_pairs={{0,1},{1,2},{2,3},{3,4},{4,5},{5,6},{6,7},{7,8},{8,9},{9,10},{10,1... | collective-permute-start | bytes 49160 | tf_op jit(solution)/shard_map/ppermute | solution.py:24
  153.0 44.8 %collective-permute-start.14 = (f32[1,1,4096]{2,1,0:T(1,128)S(1)}, f32[1,1,4096]{2,1,0:T(1,128)S(1)}, u32[]{:S(2)}, u32[]{:S(2)}) collective-permute-start(f32[1,1,4096]{2,1,0:T(1,128)S(1)} %get-tuple-element.29), channel_id=1, source_target_pairs={{1,0},{2,1},{3,2},{4,3},{5,4},{6,5},{7,6},{8,7},{9,8},{10,9},{11,1... | collective-permute-start | bytes 49160 | tf_op jit(solution)/shard_map/ppermute | solution.py:25
  156.1 41.7 %collective-permute-start.15 = (f32[1,1,4096]{2,1,0:T(1,128)S(1)}, f32[1,1,4096]{2,1,0:T(1,128)S(1)}, u32[]{:S(2)}, u32[]{:S(2)}) collective-permute-start(f32[1,1,4096]{2,1,0:T(1,128)S(1)} %get-tuple-element.28), channel_id=1, source_target_pairs={{0,1},{1,2},{2,3},{3,4},{4,5},{5,6},{6,7},{7,8},{8,9},{9,10},{10,1... | collective-permute-start | bytes 49160 | tf_op jit(solution)/shard_map/ppermute | solution.py:24
  159.6 1.7 copy-start.1
  164.9 13.0 %collective-permute-start.4 = (f32[2,1,4096]{2,1,0:T(1,128)S(1)}, f32[2,1,4096]{2,1,0:T(1,128)S(1)}, u32[]{:S(2)}, u32[]{:S(2)}) collective-permute-start(f32[2,1,4096]{2,1,0:T(1,128)S(1)} %get-tuple-element.15), channel_id=1, source_target_pairs={{1,0},{2,1},{3,2},{4,3},{5,4},{6,5},{7,6},{8,7},{9,8},{10,9},{11,1... | collective-permute-start | bytes 98312 | tf_op jit(solution)/shard_map/ppermute | solution.py:25
  170.2 9.7 %collective-permute-start.5 = (f32[2,1,4096]{2,1,0:T(1,128)S(1)}, f32[2,1,4096]{2,1,0:T(1,128)S(1)}, u32[]{:S(2)}, u32[]{:S(2)}) collective-permute-start(f32[2,1,4096]{2,1,0:T(1,128)S(1)} %get-tuple-element.14), channel_id=1, source_target_pairs={{0,1},{1,2},{2,3},{3,4},{4,5},{5,6},{6,7},{7,8},{8,9},{9,10},{10,1... | collective-permute-start | bytes 98312 | tf_op jit(solution)/shard_map/ppermute | solution.py:24
  172.2 8.6 %collective-permute-start.6 = (f32[2,1,4096]{2,1,0:T(1,128)S(1)}, f32[2,1,4096]{2,1,0:T(1,128)S(1)}, u32[]{:S(2)}, u32[]{:S(2)}) collective-permute-start(f32[2,1,4096]{2,1,0:T(1,128)S(1)} %get-tuple-element.17), channel_id=1, source_target_pairs={{1,0},{2,1},{3,2},{4,3},{5,4},{6,5},{7,6},{8,7},{9,8},{10,9},{11,1... | collective-permute-start | bytes 98312 | tf_op jit(solution)/shard_map/ppermute | solution.py:25
  177.9 6.4 %collective-permute-start.7 = (f32[2,1,4096]{2,1,0:T(1,128)S(1)}, f32[2,1,4096]{2,1,0:T(1,128)S(1)}, u32[]{:S(2)}, u32[]{:S(2)}) collective-permute-start(f32[2,1,4096]{2,1,0:T(1,128)S(1)} %get-tuple-element.16), channel_id=1, source_target_pairs={{0,1},{1,2},{2,3},{3,4},{4,5},{5,6},{6,7},{7,8},{8,9},{9,10},{10,1... | collective-permute-start | bytes 98312 | tf_op jit(solution)/shard_map/ppermute | solution.py:24
  180.7 4.5 %copy-start.6 = (f32[64,4096]{1,0:T(8,128)S(1)}, f32[64,4096]{1,0:T(8,128)}, u32[]{:S(2)}) copy-start(f32[64,4096]{1,0:T(8,128)} %param.12) | copy-start | bytes 3145732
  189.0 9.2 %collective-permute-start.8 = (f32[2,1,4096]{2,1,0:T(1,128)S(1)}, f32[2,1,4096]{2,1,0:T(1,128)S(1)}, u32[]{:S(2)}, u32[]{:S(2)}) collective-permute-start(f32[2,1,4096]{2,1,0:T(1,128)S(1)} %get-tuple-element.13), channel_id=1, source_target_pairs={{1,0},{2,1},{3,2},{4,3},{5,4},{6,5},{7,6},{8,7},{9,8},{10,9},{11,1... | collective-permute-start | bytes 98312 | tf_op jit(solution)/shard_map/ppermute | solution.py:25
  195.7 3.1 %collective-permute-start.9 = (f32[2,1,4096]{2,1,0:T(1,128)S(1)}, f32[2,1,4096]{2,1,0:T(1,128)S(1)}, u32[]{:S(2)}, u32[]{:S(2)}) collective-permute-start(f32[2,1,4096]{2,1,0:T(1,128)S(1)} %get-tuple-element.12), channel_id=1, source_target_pairs={{0,1},{1,2},{2,3},{3,4},{4,5},{5,6},{6,7},{7,8},{8,9},{9,10},{10,1... | collective-permute-start | bytes 98312 | tf_op jit(solution)/shard_map/ppermute | solution.py:24
  202.2 8.6 %collective-permute-start.12 = (f32[2,1,4096]{2,1,0:T(1,128)S(1)}, f32[2,1,4096]{2,1,0:T(1,128)S(1)}, u32[]{:S(2)}, u32[]{:S(2)}) collective-permute-start(f32[2,1,4096]{2,1,0:T(1,128)S(1)} %get-tuple-element.11), channel_id=1, source_target_pairs={{1,0},{2,1},{3,2},{4,3},{5,4},{6,5},{7,6},{8,7},{9,8},{10,9},{11,1... | collective-permute-start | bytes 98312 | tf_op jit(solution)/shard_map/ppermute | solution.py:25
  208.4 3.1 %collective-permute-start.13 = (f32[2,1,4096]{2,1,0:T(1,128)S(1)}, f32[2,1,4096]{2,1,0:T(1,128)S(1)}, u32[]{:S(2)}, u32[]{:S(2)}) collective-permute-start(f32[2,1,4096]{2,1,0:T(1,128)S(1)} %get-tuple-element.10), channel_id=1, source_target_pairs={{0,1},{1,2},{2,3},{3,4},{4,5},{5,6},{6,7},{7,8},{8,9},{9,10},{10,1... | collective-permute-start | bytes 98312 | tf_op jit(solution)/shard_map/ppermute | solution.py:24
  210.9 1.5 copy-start.7
Sparse Core Ops, SparseCore 0:
  23.2 116.5 all-reduce.10
where the time goes:
time: 281 us; the launch traced here: 280 us
  waiting for transfers between devices  111 us (40%)
  blocking collectives  56.6 us (20%)
  starting transfers between devices  54.1 us (19%)
  other arithmetic  28.8 us (10%)
  between operations  24.6 us (9%)
  local copies, waits for them, and re-layouts  4.83 us (2%)
    psum x1, waiting for transfers between devices, broadcast(): return lax.psum(block, axis)  106 us
    psum x1, blocking collectives, per_device(): summed = lax.psum(partial_sums, 'space')  56.6 us
    ppermute x8, starting transfers between devices, padded_2(): after = lax.ppermute(leading, axis, down)  34.3 us
    ppermute x8, starting transfers between devices, padded_2(): before = lax.ppermute(last, axis, up)  19.8 us
    concatenate x8, other arithmetic, padded_2(): array = jnp.concatenate([before, array, after], axis=dim)  7.33 us
  transfers between devices with their start and end apart: 17, of which 5 were waited for; matrix products, arithmetic and copies ran while one was open for 5% of the time, Pallas kernels for 0%

commit v1 on v0

v1 whole, which is shorter than its diff:
```python
import functools
import jax
import jax.numpy as jnp
from jax import lax
from jax.experimental import pallas as pl
from jax.experimental.pallas import tpu as pltpu
from jax.sharding import PartitionSpec as P

STEPS = 2
HALO = 4
TILE = 8


def pick_kernel(owners_ref, slot_ref, out_ref):
    out_ref[...] = jnp.broadcast_to(slot_ref[...][None], out_ref.shape)


def pick(owners, pieces, copies):
    slots, rows, cols = pieces.shape
    count = owners.shape[0]
    return pl.pallas_call(
        pick_kernel,
        out_shape=jax.ShapeDtypeStruct((copies, count, rows, cols), pieces.dtype),
        grid_spec=pltpu.PrefetchScalarGridSpec(
            num_scalar_prefetch=1,
            grid=(count,),
            in_specs=[pl.BlockSpec((1, rows, cols), lambda k, o: (o[k], 0, 0))],
            out_specs=pl.BlockSpec((copies, 1, rows, cols), lambda k, o: (0, k, 0, 0)),
        ),
    )(owners, pieces)


def upper(here, after):
    return jnp.concatenate([here[1:], after[:1]], axis=0)


def lower(before, here):
    return jnp.concatenate([before[-1:], here[:-1]], axis=0)


def stencil_kernel(
    edge_ref, steps_ref, rates_ref,
    dirs_hbm, ckpt_hbm, obs_hbm, prior_hbm,
    top_ref, bottom_ref, ctop_ref, cbottom_ref,
    product_hbm, curv_ref,
    state, ckpt, obs, prior, pa, qa, w1, pb, qb, out, acc, sems,
):
    dirs, rows, cols = dirs_hbm.shape
    tiles = rows // TILE
    main = pl.ds(TILE, rows)
    pieces = ckpt_hbm.shape[0]
    per = ckpt_hbm.shape[2]
    copies = [
        pltpu.make_async_copy(dirs_hbm, state.at[:, main], sems.at[0]),
        pltpu.make_async_copy(obs_hbm, obs.at[main], sems.at[1]),
        pltpu.make_async_copy(prior_hbm, prior, sems.at[2]),
    ]
    for piece in range(pieces):
        copies.append(
            pltpu.make_async_copy(
                ckpt_hbm.at[piece],
                ckpt.at[:, pl.ds(TILE + piece * per, per)],
                sems.at[3 + piece],
            )
        )
    for copy in copies:
        copy.start()
    for d in range(dirs):
        state[d, TILE - HALO:TILE] = top_ref[d]
        state[d, TILE + rows:TILE + rows + HALO] = bottom_ref[d]
    obs[TILE - HALO:TILE] = top_ref[dirs]
    obs[TILE + rows:TILE + rows + HALO] = bottom_ref[dirs]
    for k in range(2 * STEPS):
        ckpt[k, TILE - HALO:TILE] = ctop_ref[k]
        ckpt[k, TILE + rows:TILE + rows + HALO] = cbottom_ref[k]
    for copy in copies:
        copy.wait()
    r0 = rates_ref[steps_ref[0]]
    r1 = rates_ref[steps_ref[1]]
    s0 = 1.0 - 4.0 * r0
    s1 = 1.0 - 4.0 * r1
    has_top = edge_ref[0]
    has_bottom = edge_ref[1]
    column = lax.broadcasted_iota(jnp.int32, (TILE, cols), 1)
    first = column == 0
    last = column == cols - 1

    def right(x):
        return jnp.where(last, 0.0, pltpu.roll(x, cols - 1, 1))

    def left(x):
        return jnp.where(first, 0.0, pltpu.roll(x, 1, 1))

    def inside(t, x):
        keep = jnp.logical_or(
            jnp.logical_and(t > 0, t < tiles + 1),
            jnp.where(t == 0, has_top, has_bottom) > 0,
        )
        return jnp.where(keep, x, 0.0)

    def rows_of(t):
        return pl.ds(pl.multiple_of(t * TILE, TILE), TILE)

    def around(t):
        return (
            rows_of(jnp.maximum(t - 1, 0)),
            rows_of(t),
            rows_of(jnp.minimum(t + 1, tiles + 1)),
        )

    def first_pass(t, _):
        r = rows_of(t)
        lift = 0.125 * ckpt[0, r]
        for d in range(dirs):
            v = state[d, r]
            pa[d, r] = v * (r0 - lift)
            qa[d, r] = v * (r0 + lift)
        return 0

    def advance(t, scale, base, p, q, d):
        b, r, a = around(t)
        here_p = p[d, r]
        here_q = q[d, r]
        return (
            scale * base[d, r]
            + upper(here_p, p[d, a])
            + lower(q[d, b], here_q)
            + right(here_p)
            + left(here_q)
        )

    def second_pass(t, _):
        r = rows_of(t)
        lift = 0.125 * ckpt[1, r]
        for d in range(dirs):
            w = inside(t, advance(t, s0, state, pa, qa, d))
            w1[d, r] = w
            pb[d, r] = w * (r1 - lift)
            qb[d, r] = w * (r1 + lift)
        return 0

    def third_pass(t, _):
        r = rows_of(t)
        for d in range(dirs):
            w = inside(t, advance(t, s1, w1, pb, qb, d))
            pa[d, r] = obs[r] * w
        return 0

    def pull(t, rate, scale, vel, adj, hist, q, d):
        b, r, a = around(t)
        lift = 0.125 * ckpt[vel, r]
        slope = ckpt[adj, r]
        slope = 0.125 * (
            upper(slope, ckpt[adj, a]) - lower(ckpt[adj, b], slope) + right(slope) - left(slope)
        )
        here = q[d, r]
        return (
            scale * here
            + (rate + lift) * (upper(here, q[d, a]) + right(here))
            + (rate - lift) * (lower(q[d, b], here) + left(here))
            + hist[d, r] * slope
        )

    def fourth_pass(t, _):
        r = rows_of(t)
        for d in range(dirs):
            qa[d, r] = inside(t, pull(t, r1, s1, 1, 3, w1, pa, d))
        return 0

    def fifth_pass(t, _):
        r = rows_of(t)
        o = rows_of(t - 1)
        for d in range(dirs):
            v = state[d, r]
            value = pull(t, r0, s0, 0, 2, state, qa, d) + prior[o] * v
            out[d, o] = value
            acc[d] += v * value
        return 0

    acc[...] = jnp.zeros_like(acc)
    lax.fori_loop(0, tiles + 2, first_pass, 0)
    lax.fori_loop(0, tiles + 2, second_pass, 0)
    lax.fori_loop(0, tiles + 2, third_pass, 0)
    lax.fori_loop(0, tiles + 2, fourth_pass, 0)
    lax.fori_loop(1, tiles + 1, fifth_pass, 0)
    done = pltpu.make_async_copy(out, product_hbm, sems.at[0])
    done.start()
    for d in range(dirs):
        total = jnp.sum(acc[d], axis=(0, 1), keepdims=True)
        curv_ref[pl.ds(d, 1), :] = jnp.broadcast_to(total, (1, 128))
    done.wait()


def stencil(edge, steps, diffusion, dirs, ckpt, obs, prior, top, bottom, ctop, cbottom):
    count, rows, cols = dirs.shape
    ext = rows + 2 * TILE
    vmem = pl.BlockSpec(memory_space=pltpu.VMEM)
    smem = pl.BlockSpec(memory_space=pltpu.SMEM)
    anywhere = pl.BlockSpec(memory_space=pl.ANY)
    f32 = jnp.float32
    return pl.pallas_call(
        stencil_kernel,
        out_shape=(
            jax.ShapeDtypeStruct(dirs.shape, f32),
            jax.ShapeDtypeStruct((count, 128), f32),
        ),
        in_specs=[smem] * 3 + [anywhere] * 4 + [vmem] * 4,
        out_specs=(anywhere, vmem),
        scratch_shapes=[
            pltpu.VMEM((count, ext, cols), f32),
            pltpu.VMEM((2 * STEPS, ext, cols), f32),
            pltpu.VMEM((ext, cols), f32),
            pltpu.VMEM((rows, cols), f32),
        ]
        + [pltpu.VMEM((count, ext, cols), f32)] * 5
        + [
            pltpu.VMEM((count, rows, cols), f32),
            pltpu.VMEM((count, TILE, cols), f32),
            pltpu.SemaphoreType.DMA((3 + ckpt.shape[0],)),
        ],
        compiler_params=pltpu.CompilerParams(vmem_limit_bytes=60 * 1024 * 1024),
    )(edge, steps, diffusion, dirs, ckpt, obs, prior, top, bottom, ctop, cbottom)


def per_device(directions, pool, owners, window_steps, diffusion, obs_weight, prior_diag):
    peers = lax.axis_size("space")
    groups = lax.axis_size("dir")
    here = lax.axis_index("space")
    up = [(i, i + 1) for i in range(peers - 1)]
    down = [(j, i) for i, j in up]

    def halos(main):
        before = lax.ppermute(main[1], "space", up)
        after = lax.ppermute(main[0], "space", down)
        return before, after

    edge_first = jnp.concatenate([directions[:, :HALO], obs_weight[None, :HALO]], axis=0)
    edge_last = jnp.concatenate([directions[:, -HALO:], obs_weight[None, -HALO:]], axis=0)
    top, bottom = halos((edge_first, edge_last))

    pieces = lax.all_to_all(pool, "dir", 1, 0, tiled=True)
    chosen = pick(owners.reshape(-1), pieces, groups)
    ckpt = lax.all_to_all(chosen, "dir", 0, 0, tiled=True)
    ctop, cbottom = halos((ckpt[0, :, :HALO], ckpt[groups - 1, :, -HALO:]))

    edge = jnp.stack([here > 0, here < peers - 1]).astype(jnp.int32)
    product, partial_sums = stencil(
        edge, window_steps, diffusion, directions, ckpt, obs_weight, prior_diag,
        top, bottom, ctop, cbottom,
    )
    spread = jnp.broadcast_to(partial_sums[None], (peers,) + partial_sums.shape)
    gathered = lax.all_to_all(spread, "space", 0, 0, tiled=True)
    summed = jnp.sum(gathered, axis=0)[:, 0]
    cells = directions.shape[1] * peers * directions.shape[2]
    return (product, summed / cells)


def solution(mesh):
    return jax.shard_map(
        per_device,
        mesh=mesh,
        in_specs=(
            P("dir", "space", None),
            P("dir", "space", None),
            P(),
            P(),
            P(),
            P("space", None),
            P("space", None),
        ),
        out_specs=(P("dir", "space", None), P("dir")),
        check_vma=False,
    )
```

time: 281 us -> 157 us (0.56)
  the two profiles are of different devices: /device:TPU:129 before, /device:TPU:1 now
where the time goes in v1:
time: 157 us; the launch traced here: 156 us
  waiting for transfers between devices  74.3 us (47%)
  starting transfers between devices  23.1 us (15%)
  Pallas kernels  22.9 us (15%)
  blocking collectives  20.8 us (13%)
  local copies, waits for them, and re-layouts  13.1 us (8%)
    all_to_all x1, waiting for transfers between devices, per_device(): ckpt = lax.all_to_all(chosen, 'dir', 0, 0, tiled=True)  43.8 us
    all_to_all x1, waiting for transfers between devices, per_device(): pieces = lax.all_to_all(pool, 'dir', 1, 0, tiled=True)  25.6 us
    all_to_all x1, blocking collectives, per_device(): gathered = lax.all_to_all(spread, 'space', 0, 0, tiled=True)  20.8 us
    pallas_call x1, Pallas kernels, stencil(): pl.pallas_call(stencil_kernel, out_shape=(jax.ShapeDtypeStruct(dirs.shape...  18.3 us
    all_to_all x1, starting transfers between devices, per_device(): pieces = lax.all_to_all(pool, 'dir', 1, 0, tiled=True)  7.6 us
    ppermute x2, starting transfers between devices, halos(): before = lax.ppermute(main[1], 'space', up)  6.15 us
    unnamed x11, local copies, waits for them, and re-layouts  5.99 us
    all_to_all x1, starting transfers between devices, per_device(): ckpt = lax.all_to_all(chosen, 'dir', 0, 0, tiled=True)  5.16 us
  transfers between devices with their start and end apart: 6, of which 3 were waited for; matrix products, arithmetic and copies ran while one was open for 3% of the time, Pallas kernels for 0%

profile of v1, /device:TPU:1, one launch (start us, length us, event | category | flops | bytes accessed | tf_op | source)
XLA Modules:
  0.0 156.3 jit_solution(10068665964695017939)
XLA Ops:
  0.6 4.5 %copy.16 = f32[2,64,4096]{2,0,1:T(2,128)} copy(f32[2,64,4096]{2,1,0:T(8,128)} %param.8) | data formatting | bytes 4194304 | tf_op args[1]
  5.2 0.0 copy-start.4
  5.2 7.6 %all-to-all-start = ((f32[2,64,4096]{2,0,1:T(2,128)}), f32[2,64,4096]{2,0,1:T(2,128)S(1)}, u32[]{:S(2)}, u32[]{:S(2)}) async-start(f32[2,64,4096]{2,0,1:T(2,128)} %copy.16), calls=%async_computation | async-start | bytes 4194304 | tf_op jit(solution)/shard_map/all_to_all | solution.py:241
  12.8 0.0 copy-done.4
  12.8 0.6 reshape.10.owners_ref
  13.4 25.6 %all-to-all-done = f32[2,64,4096]{2,0,1:T(2,128)S(1)} async-done(((f32[2,64,4096]{2,0,1:T(2,128)}), f32[2,64,4096]{2,0,1:T(2,128)S(1)}, u32[]{:S(2)}, u32[]{:S(2)}) %all-to-all-start) | async-done | bytes 2097184 | tf_op jit(solution)/shard_map/all_to_all | solution.py:241
  39.0 2.5 %copy.17 = f32[2,8,8,4096]{3,2,0,1:T(8,128)} copy(f32[2,8,8,4096]{3,0,2,1:T(2,128)S(1)} %bitcast.15) | data formatting | bytes 4194304 | tf_op jit(solution)/shard_map/all_to_all | solution.py:241
  41.5 4.6 %shard_map.86 = f32[8,4,8,4096]{3,2,1,0:T(8,128)} custom-call(s32[4]{0:T(128)} %reshape.10.owners_ref, f32[16,8,4096]{2,1,0:T(8,128)} %bitcast.14), custom_call_target="tpu_custom_call" | custom-call | tf_op jit(solution)/shard_map/pallas_call | solution.py:21
  46.1 5.2 %all-to-all-start.1 = ((f32[8,4,8,4096]{3,2,1,0:T(8,128)}), f32[8,4,8,4096]{3,2,1,0:T(8,128)}, u32[]{:S(2)}, u32[]{:S(2)}) async-start(f32[8,4,8,4096]{3,2,1,0:T(8,128)} %shard_map.86), calls=%async_computation.1 | async-start | bytes 8388608 | tf_op jit(solution)/shard_map/all_to_all | solution.py:243
  51.2 1.0 slice_bitcast_fusion.2
  52.2 1.1 fusion
  53.4 2.9 %collective-permute-start = (f32[3,4,4096]{2,1,0:T(4,128)S(1)}, f32[3,4,4096]{2,1,0:T(4,128)S(1)}, u32[]{:S(2)}, u32[]{:S(2)}) collective-permute-start(f32[3,4,4096]{2,1,0:T(4,128)S(1)} %pad_maximum_fusion), channel_id=1, source_target_pairs={{0,1},{1,2},{2,3},{3,4},{4,5},{5,6},{6,7},{7,8},{8,9},{9,10},{10,1... | collective-permute-start | bytes 589832 | tf_op jit(solution)/shard_map/ppermute | solution.py:233
  56.3 43.8 %all-to-all-done.1.ckpt_hbm = f32[8,4,8,4096]{3,2,1,0:T(8,128)} async-done(((f32[8,4,8,4096]{3,2,1,0:T(8,128)}), f32[8,4,8,4096]{3,2,1,0:T(8,128)}, u32[]{:S(2)}, u32[]{:S(2)}) %all-to-all-start.1) | async-done | bytes 4194336 | tf_op jit(solution)/shard_map/all_to_all | solution.py:243
  100.0 1.3 slice_bitcast_fusion
  101.3 3.3 %collective-permute-start.2 = (f32[4,4,4096]{2,1,0:T(4,128)S(1)}, f32[4,4,4096]{2,1,0:T(4,128)S(1)}, u32[]{:S(2)}, u32[]{:S(2)}) collective-permute-start(f32[4,4,4096]{2,1,0:T(4,128)S(1)} %get-tuple-element.7), channel_id=1, source_target_pairs={{0,1},{1,2},{2,3},{3,4},{4,5},{5,6},{6,7},{7,8},{8,9},{9,10},{10,1... | collective-permute-start | bytes 786440 | tf_op jit(solution)/shard_map/ppermute | solution.py:233
  104.6 2.3 %collective-permute-start.3 = (f32[4,4,4096]{2,1,0:T(4,128)S(1)}, f32[4,4,4096]{2,1,0:T(4,128)S(1)}, u32[]{:S(2)}, u32[]{:S(2)}) collective-permute-start(f32[4,4,4096]{2,1,0:T(4,128)S(1)} %get-tuple-element.6), channel_id=1, source_target_pairs={{1,0},{2,1},{3,2},{4,3},{5,4},{6,5},{7,6},{8,7},{9,8},{10,9},{11,1... | collective-permute-start | bytes 786440 | tf_op jit(solution)/shard_map/ppermute | solution.py:234
  106.9 1.9 %collective-permute-start.1 = (f32[3,4,4096]{2,1,0:T(4,128)S(1)}, f32[3,4,4096]{2,1,0:T(4,128)S(1)}, u32[]{:S(2)}, u32[]{:S(2)}) collective-permute-start(f32[3,4,4096]{2,1,0:T(4,128)S(1)} %pad_maximum_fusion.1), channel_id=1, source_target_pairs={{1,0},{2,1},{3,2},{4,3},{5,4},{6,5},{7,6},{8,7},{9,8},{10,9},{11,1... | collective-permute-start | bytes 589832 | tf_op jit(solution)/shard_map/ppermute | solution.py:234
  108.9 0.6 add_convert_fusion.edge_ref
  109.5 0.0 collective-permute-done.top_ref
  109.5 0.0 copy-start.2
  109.5 4.9 %collective-permute-done.1.bottom_ref = f32[3,4,4096]{2,1,0:T(4,128)S(1)} collective-permute-done((f32[3,4,4096]{2,1,0:T(4,128)S(1)}, f32[3,4,4096]{2,1,0:T(4,128)S(1)}, u32[]{:S(2)}, u32[]{:S(2)}) %collective-permute-start.1) | collective-permute-done | bytes 196640 | tf_op jit(solution)/shard_map/ppermute | solution.py:234
  114.4 0.0 copy-start.3
  114.4 0.0 collective-permute-done.2.ctop_ref
  114.4 0.0 collective-permute-done.3.cbottom_ref
  114.4 0.0 copy-done.2
  114.4 0.7 copy-done.3
  115.1 0.1 copy-done
  115.2 0.7 copy-done.1
  115.9 18.3 %shard_map.87 = (f32[2,64,4096]{2,1,0:T(8,128)}, f32[2,128]{1,0:T(2,128)}) custom-call(s32[2]{0:T(128)} %add_convert_fusion.edge_ref, s32[2]{0:T(128)} %steps_ref.1, f32[512]{0:T(512)} %rates_ref.1, f32[2,64,4096]{2,1,0:T(8,128)} %dirs_hbm.1, f32[8,4,8,4096]{3,2,1,0:T(8,128)} %all-to-all-done.1.ckpt_hbm, f32[64,4096]{1,0:T(8,128)} %obs_hbm.1, ...), custom_call_target="tpu_custom_call" | custom-call | tf_op jit(solution)/shard_map/pallas_call | solution.py:201
  134.2 0.6 broadcast_in_dim.14
  134.8 20.8 %all_to_all.28 = f32[32,2,128]{2,1,0:T(2,128)S(1)} all-to-all(f32[32,2,128]{2,1,0:T(2,128)S(1)} %broadcast_in_dim.14), channel_id=1, replica_groups=mesh['dir'=8,'space'=32] {'space'}, dimensions={0} | all-to-all | bytes 65536 | tf_op jit(solution)/shard_map/all_to_all | solution.py:252
  155.7 0.6 multiply_reduce_fusion
  (5 shorter events, 0.1 us)
Async XLA Ops:
  5.2 7.6 %copy-start.4 = (s32[2,2]{1,0:T(2,128)S(1)}, s32[2,2]{1,0:T(2,128)}, u32[]{:S(2)}) copy-start(s32[2,2]{1,0:T(2,128)} %param.9) | copy-start | bytes 52
  5.2 33.8 %all-to-all-start = ((f32[2,64,4096]{2,0,1:T(2,128)}), f32[2,64,4096]{2,0,1:T(2,128)S(1)}, u32[]{:S(2)}, u32[]{:S(2)}) async-start(f32[2,64,4096]{2,0,1:T(2,128)} %copy.16), calls=%async_computation | async-start | bytes 4194304 | tf_op jit(solution)/shard_map/all_to_all | solution.py:241
  46.1 53.9 %all-to-all-start.1 = ((f32[8,4,8,4096]{3,2,1,0:T(8,128)}), f32[8,4,8,4096]{3,2,1,0:T(8,128)}, u32[]{:S(2)}, u32[]{:S(2)}) async-start(f32[8,4,8,4096]{3,2,1,0:T(8,128)} %shard_map.86), calls=%async_computation.1 | async-start | bytes 8388608 | tf_op jit(solution)/shard_map/all_to_all | solution.py:243
  53.4 56.1 %collective-permute-start = (f32[3,4,4096]{2,1,0:T(4,128)S(1)}, f32[3,4,4096]{2,1,0:T(4,128)S(1)}, u32[]{:S(2)}, u32[]{:S(2)}) collective-permute-start(f32[3,4,4096]{2,1,0:T(4,128)S(1)} %pad_maximum_fusion), channel_id=1, source_target_pairs={{0,1},{1,2},{2,3},{3,4},{4,5},{5,6},{6,7},{7,8},{8,9},{9,10},{10,1... | collective-permute-start | bytes 589832 | tf_op jit(solution)/shard_map/ppermute | solution.py:233
  101.3 13.1 %collective-permute-start.2 = (f32[4,4,4096]{2,1,0:T(4,128)S(1)}, f32[4,4,4096]{2,1,0:T(4,128)S(1)}, u32[]{:S(2)}, u32[]{:S(2)}) collective-permute-start(f32[4,4,4096]{2,1,0:T(4,128)S(1)} %get-tuple-element.7), channel_id=1, source_target_pairs={{0,1},{1,2},{2,3},{3,4},{4,5},{5,6},{6,7},{7,8},{8,9},{9,10},{10,1... | collective-permute-start | bytes 786440 | tf_op jit(solution)/shard_map/ppermute | solution.py:233
  104.6 9.8 %collective-permute-start.3 = (f32[4,4,4096]{2,1,0:T(4,128)S(1)}, f32[4,4,4096]{2,1,0:T(4,128)S(1)}, u32[]{:S(2)}, u32[]{:S(2)}) collective-permute-start(f32[4,4,4096]{2,1,0:T(4,128)S(1)} %get-tuple-element.6), channel_id=1, source_target_pairs={{1,0},{2,1},{3,2},{4,3},{5,4},{6,5},{7,6},{8,7},{9,8},{10,9},{11,1... | collective-permute-start | bytes 786440 | tf_op jit(solution)/shard_map/ppermute | solution.py:234
  106.9 7.5 %collective-permute-start.1 = (f32[3,4,4096]{2,1,0:T(4,128)S(1)}, f32[3,4,4096]{2,1,0:T(4,128)S(1)}, u32[]{:S(2)}, u32[]{:S(2)}) collective-permute-start(f32[3,4,4096]{2,1,0:T(4,128)S(1)} %pad_maximum_fusion.1), channel_id=1, source_target_pairs={{1,0},{2,1},{3,2},{4,3},{5,4},{6,5},{7,6},{8,7},{9,8},{10,9},{11,1... | collective-permute-start | bytes 589832 | tf_op jit(solution)/shard_map/ppermute | solution.py:234
  109.5 4.9 %copy-start.2 = (f32[3,4,4096]{2,1,0:T(4,128)}, f32[3,4,4096]{2,1,0:T(4,128)S(1)}, u32[]{:S(2)}) copy-start(f32[3,4,4096]{2,1,0:T(4,128)S(1)} %collective-permute-done.top_ref) | copy-start | bytes 589828
  114.4 0.7 copy-start.3
  114.4 0.8 copy-start
  115.2 0.7 copy-start.1
